TPU v7x, 32 devices: a whole 2x2x4 slice. The times are simulated.
32 devices in a mesh: dp: 2 (over core), ctx: 4 (over z), vocab: 4 (over y, x).
Axes of the slice: x: 2, y: 2, z: 4, core: 2. Of those that a mesh axis runs over, the one named last changes fastest.
Arguments:
- hidden: bfloat16 [512, 4096], P(('dp', 'ctx')), may hold values from -32 to 32
- head_weight: bfloat16 [4096, 9504], P(None, ('ctx', 'vocab')), may hold values from -2 to 2
- targets: int32 [512], P('dp'), may hold values from 0 to 9503
- segment_ids: int32 [512], P('dp'), may hold values from 0 to 31, as said below
- lengths: int32 [32], replicated, may hold values from 8 to 24, as said below
- loss_mask: int32 [512], P('dp'), may hold values 0 or 1
- advantages: float32 [32], replicated, may hold values from -4 to 4
- ref_logprobs: float32 [512], P('dp'), may hold values from -40 to -2
Outputs:
- grad_hidden: bfloat16 [512, 4096], P(('dp', 'ctx', 'vocab'))
- grad_head: bfloat16 [4096, 9504], P(None, ('ctx', 'vocab'))
Inputs may be any that keep to these rules, and one draw needn't show every extreme that they name: `segment_ids`: each sequence's tokens are contiguous; the tokens b * 64 to (b + 1) * 64 - 1 carry ids b * 4 to (b + 1) * 4 - 1, never falling, each id used. lengths[s] is the number of tokens whose segment id is s.
All inputs are finite; a program needn't handle non-finite values. No bound on the sum of `loss_mask` on one device may be relied on, other than what follows from the above.
Results may differ from a plain program's by a relative error of at most 0.012.
Values may be sent and summed in bfloat16 or wider, within the bound.
A program may use at most 128 MiB of HBM per device.

v0:
```python
import jax
import jax.numpy as jnp
from jax import lax
from jax.sharding import PartitionSpec as P

LOSS_SCALE = 1024


kl_weight = 0.1
entropy_weight = 0.05


def per_device(
    hidden, head_weight, targets, segment_ids, lengths, loss_mask, advantages, ref_logprobs
):
    vocab_width = head_weight.shape[1]
    first_column = (
        lax.axis_index("ctx") * lax.axis_size("vocab") + lax.axis_index("vocab")
    ) * vocab_width
    gathered = lax.all_gather(hidden, "ctx", axis=0, tiled=True)
    logits = jnp.dot(gathered, head_weight, preferred_element_type=jnp.float32)
    columns = first_column + lax.iota(jnp.int32, vocab_width)
    target_hits = targets[:, None] == columns[None, :]
    target_part = jnp.sum(jnp.where(target_hits, logits, 0.0), axis=1)
    row_max = lax.pmax(jnp.max(logits, axis=1), ("ctx", "vocab"))
    shifted = jnp.exp(logits - row_max[:, None])
    exp_total, exp_logit, target_logit = lax.psum(
        (jnp.sum(shifted, axis=1), jnp.sum(shifted * logits, axis=1), target_part), ("ctx", "vocab")
    )
    log_total = row_max + jnp.log(exp_total)
    target_logp = target_logit - log_total
    mean_logit = exp_logit / exp_total
    probs = jnp.exp(logits - log_total[:, None])
    seq_onehot = segment_ids[:, None] == lax.iota(jnp.int32, advantages.shape[0])[None, :]
    token_adv = jnp.sum(jnp.where(seq_onehot, advantages[None, :], 0.0), axis=1)
    token_len = jnp.sum(jnp.where(seq_onehot, lengths[None, :].astype(jnp.float32), 0.0), axis=1)
    token_weight = LOSS_SCALE * loss_mask.astype(jnp.float32) / token_len
    logp_grad = -token_adv + kl_weight * (target_logp - ref_logprobs)
    inner = logp_grad[:, None] * (target_hits.astype(jnp.float32) - probs)
    inner = inner + entropy_weight * probs * (logits - mean_logit[:, None])
    grad_logits = (token_weight[:, None] * inner).astype(jnp.bfloat16)
    head_local = lax.dot_general(
        gathered, grad_logits, (((0,), (0,)), ((), ())), preferred_element_type=jnp.float32
    ).astype(jnp.bfloat16)
    grad_head = lax.psum(head_local, "dp").astype(jnp.float32).astype(jnp.bfloat16)
    grad_hidden = lax.psum_scatter(
        lax.dot_general(
            grad_logits, head_weight, (((1,), (1,)), ((), ())), preferred_element_type=jnp.float32
        ),
        ("ctx", "vocab"),
        scatter_dimension=0,
        tiled=True,
    )
    return (grad_hidden.astype(jnp.bfloat16), grad_head)


def solution(mesh):
    return jax.shard_map(
        per_device,
        mesh=mesh,
        in_specs=(
            P(("dp", "ctx"), None),
            P(None, ("ctx", "vocab")),
            P("dp"),
            P("dp"),
            P(),
            P("dp"),
            P(),
            P("dp"),
        ),
        out_specs=(P(("dp", "ctx", "vocab"), None), P(None, ("ctx", "vocab"))),
        check_vma=False,
    )
```

profile of v0, /device:TPU:0, one launch (start us, length us, event | category | flops | bytes accessed | tf_op | source)
XLA Modules:
  0.0 282.1 jit_solution(3857916356808033694)
XLA Ops:
  7.2 0.0 all-gather.2.cloned.1.call-start
  7.2 0.7 all-gather.2.cloned.1.call-update
  7.9 0.0 reduce-scatter.2.cloned.1.call-start
  7.9 0.7 convert_element_type.25
  8.6 0.8 select_reduce_fusion.1
  9.4 0.7 multiply_divide_fusion
  10.1 0.0 copy-start.1
  10.1 47.9 %all-gather.2.cloned.1.call-done = bf16[256,4096]{1,0:T(8,128)(2,1)} async-done(((bf16[64,4096]{1,0:T(8,128)(2,1)}), bf16[256,4096]{1,0:T(8,128)(2,1)}) %all-gather.2.cloned.1.call-update) | async-done | bytes 2097168 | tf_op jit(solution)/shard_map/all_gather | solution.py:20
  58.0 4.5 %fusion.11 = (f32[256]{0:T(256)S(1)}, f32[256,594]{0,1:T(8,128)S(1)}) fusion(bf16[256,4096]{1,0:T(8,128)(2,1)} %all-gather.2.cloned.1.call-done, bf16[4096,594]{0,1:T(8,128)(2,1)} %param.9), kind=kOutput, calls=%fused_computation.21 | convolution fusion | flops 1245860096 | bytes 7572480 | tf_op jit(solution)/shard_map/dot_general | solution.py:21
  62.5 39.5 %pmax.7 = f32[256]{0:T(256)S(1)} all-reduce(f32[256]{0:T(256)S(1)} %get-tuple-element.13), channel_id=1, replica_groups=mesh['dp'=2,'ctx'=4,'vocab'=4] {'ctx','vocab'}, use_global_device_ids=true, to_apply=%region_5.6 | all-reduce | flops 256 | bytes 2048 | tf_op jit(solution)/shard_map/pmax | solution.py:25
  102.0 0.0 copy-done.1
  102.0 0.2 fusion.7
  102.2 36.6 %all-reduce = (f32[256]{0:T(256)S(1)}, f32[256]{0:T(256)S(1)}, f32[256]{0:T(256)S(1)}) all-reduce(f32[256]{0:T(256)S(1)} %get-tuple-element.3, f32[256]{0:T(256)S(1)} %get-tuple-element.2, f32[256]{0:T(256)S(1)} %get-tuple-element.4), channel_id=1, replica_groups=mesh['dp'=2,'ctx'=4,'vocab'=4] {'ctx','vocab'}, use_global_device_ids=true, to_apply=%region_9.10 | all-reduce | flops 768 | bytes 6144 | tf_op jit(solution)/shard_map/psum | solution.py:27
  138.8 0.0 copy-done.2
  138.8 6.5 %fusion.9 = f32[256,4096]{1,0:T(8,128)} fusion(bf16[4096,594]{0,1:T(8,128)(2,1)} %param.9, f32[256,594]{0,1:T(8,128)S(1)} %get-tuple-element.14, f32[256]{0:T(256)S(1)} %get-tuple-element.12, f32[256]{0:T(256)S(1)} %get-tuple-element.11, f32[256]{0:T(256)S(1)} %get-tuple-element.10, s32[256]{0:T(256)S(1)} %copy-done.1, f32[256]{0:T(256)S(1)} %multiply_divide_fusion, ...), kind=kOutput, calls=%fused_computation.20 | convolution fusion | flops 1247380992 | bytes 9676104 | tf_op jit(solution)/shard_map/dot_general | solution.py:47
  145.3 0.0 reduce-scatter.2.cloned.1.call-update
  145.3 0.0 all-reduce.3.cloned.1.call-start
  145.4 1.5 copy-done
  146.9 3.9 %fusion = bf16[4096,594]{0,1:T(8,128)(2,1)} fusion(bf16[256,4096]{1,0:T(8,128)(2,1)S(1)} %copy-done, f32[256,594]{0,1:T(8,128)S(1)} %get-tuple-element.14, f32[256]{0:T(256)S(1)} %get-tuple-element.12, f32[256]{0:T(256)S(1)} %get-tuple-element.11, f32[256]{0:T(256)S(1)} %get-tuple-element.10, s32[256]{0:T(256)S(1)} %copy-done.1, ...), kind=kOutput, calls=%fused_computation.1 | convolution fusion | flops 1249814016 | bytes 7578952 | tf_op jit(solution)/shard_map/dot_general | solution.py:42
  150.7 0.0 all-reduce.3.cloned.1.call-update
  150.8 87.7 %reduce-scatter.2.cloned.1.call-done = f32[16,4096]{1,0:T(8,128)} async-done(((f32[256,4096]{1,0:T(8,128)}), f32[16,4096]{1,0:T(8,128)}) %reduce-scatter.2.cloned.1.call-update) | async-done | bytes 262160 | tf_op jit(solution)/shard_map/reduce_scatter | solution.py:46
  238.5 1.6 convert_element_type.28
  240.1 30.2 %all-reduce.3.cloned.1.call-done = bf16[4096,594]{0,1:T(8,128)(2,1)} async-done(((bf16[4096,594]{0,1:T(8,128)(2,1)}), bf16[4096,594]{0,1:T(8,128)(2,1)}) %all-reduce.3.cloned.1.call-update) | async-done | bytes 4866064 | tf_op jit(solution)/shard_map/psum | solution.py:45
  270.3 5.2 %copy.11 = bf16[4096,594]{0,1:T(8,128)(2,1)} copy(bf16[4096,594]{0,1:T(8,128)(2,1)} %all-reduce.3.cloned.1.call-done) | data formatting | bytes 9732096
  (4 shorter events, 0.0 us)
Async XLA Ops:
  7.2 50.8 %all-gather.2.cloned.1.call-start = ((), (), s32[]{:S(2)}) async-start(), calls=%async_computation.1 | async-start | bytes 2621440 | tf_op jit(solution)/shard_map/all_gather | solution.py:20
  7.9 230.6 %reduce-scatter.2.cloned.1.call-start = ((), (), s32[]{:S(2)}) async-start(), calls=%async_computation.2 | async-start | bytes 4456448 | tf_op jit(solution)/shard_map/reduce_scatter | solution.py:46
  10.1 91.9 %copy-start.1 = (s32[256]{0:T(256)S(1)}, s32[256]{0:T(256)}, u32[]{:S(2)}) copy-start(s32[256]{0:T(256)} %param.10) | copy-start | bytes 3076
  10.1 128.7 %copy-start.2 = (f32[256]{0:T(256)S(1)}, f32[256]{0:T(256)}, u32[]{:S(2)}) copy-start(f32[256]{0:T(256)} %param.15) | copy-start | bytes 3076
  145.3 1.6 copy-start
  145.3 125.0 %all-reduce.3.cloned.1.call-start = ((), (), s32[]{:S(2)}) async-start(), calls=%async_computation.3 | async-start | bytes 9830400 | tf_op jit(solution)/shard_map/psum | solution.py:45
Sparse Core Ops, SparseCore 0:
  9.5 48.3 all-gather.1
  145.4 93.0 reduce-scatter.1
  241.6 28.6 all-reduce.2
where the time goes:
time: 282 us
  waiting for transfers between devices  167 us (59%)
  blocking collectives  76.1 us (27%)
  matrix products  14.9 us (5%)
  between operations  13.8 us (5%)
  local copies, waits for them, and re-layouts  6.77 us (2%)
  other arithmetic  3.95 us (1%)
    reduce_scatter x1, waiting for transfers between devices, per_device(): lax.psum_scatter(lax.dot_general(grad_logits, head_weight, (((1,), (1,)),...  87.7 us
    all_gather x1, waiting for transfers between devices, per_device(): gathered = lax.all_gather(hidden, 'ctx', axis=0, tiled=True)  47.9 us
    pmax x1, blocking collectives, per_device(): row_max = lax.pmax(jnp.max(logits, axis=1), ('ctx', 'vocab'))  39.5 us
    psum x1, blocking collectives, per_device(): lax.psum((jnp.sum(shifted, axis=1), jnp.sum(shifted * logits, axis=1), ta...  36.6 us
    psum x1, waiting for transfers between devices, per_device(): lax.psum(head_local, 'dp').astype(jnp.float32).astype(jnp.bfloat16)  30.2 us
    unnamed x7, local copies, waits for them, and re-layouts  6.77 us
    dot_general x1, matrix products, per_device(): lax.dot_general(grad_logits, head_weight, (((1,), (1,)), ((), ())), prefe...  6.48 us
  transfers between devices with their start and end apart: 3, of which 3 were waited for; matrix products, arithmetic and copies ran while one was open for 3% of the time, Pallas kernels for 0%

commit v1 on v0

v1 whole, which is shorter than its diff:
```python
import functools

import jax
import jax.numpy as jnp
from jax import lax
from jax.experimental import pallas as pl
from jax.experimental.pallas import tpu as pltpu
from jax.sharding import PartitionSpec as P

LOSS_SCALE = 1024


kl_weight = 0.1
entropy_weight = 0.05
MESH = pl.DeviceIdType.MESH
CHUNKS = 4
STATS = 8


def combine(parts):
    top = functools.reduce(jnp.maximum, [p[0:1] for p in parts])
    scales = [jnp.exp(p[0:1] - top) for p in parts]
    total = sum(p[1:2] * s for p, s in zip(parts, scales))
    logit = sum(p[2:3] * s for p, s in zip(parts, scales))
    target = sum(p[3:4] for p in parts)
    return top, total, logit, target


def kernel(
    n_dp, n_ctx, n_vocab,
    hid, head, lengths, advantages, targets, segments, mask, ref_lp,
    rows_out, hid_all, grad_all,
    weight, hbuf, logits, rowbuf, colbuf, tcol, statcol, stat_own, stat_mid, stat_v, stat_c,
    gbuf, pbuf, part_v, sums, part_c,
    local_sem, z_send, z_recv, x_send, x_recv, d_send, d_recv, g_send, g_recv,
    sv_send, sv_recv, sc_send, sc_recv, a_send, a_recv, b_send, b_recv,
):
    g, c, v = lax.axis_index("dp"), lax.axis_index("ctx"), lax.axis_index("vocab")
    block, depth = hid.shape
    tokens, width = logits.shape
    quarter = depth // n_vocab
    chunk = depth // CHUNKS
    out_rows = rows_out.shape[0]

    def up(axis, n, step):
        return lax.rem(axis + step, n)

    def down(axis, n, step):
        return lax.rem(axis + n - step, n)

    def remote(src, dst, send, recv, where):
        copy = pltpu.make_async_remote_copy(
            src_ref=src, dst_ref=dst, send_sem=send, recv_sem=recv,
            device_id=where, device_id_type=MESH,
        )
        return copy

    load_w = pltpu.make_async_copy(head, weight, local_sem.at[0])
    load_w.start()
    own_rows = pl.ds(pl.multiple_of(c * block, block), block)
    load_h = pltpu.make_async_copy(hid, hbuf.at[own_rows], local_sem.at[1])
    load_h.start()

    barrier = pltpu.get_barrier_semaphore()
    for step in range(1, n_ctx):
        pl.semaphore_signal(barrier, inc=1, device_id=(g, up(c, n_ctx, step), v), device_id_type=MESH)
    for step in range(1, n_vocab):
        pl.semaphore_signal(barrier, inc=1, device_id=(g, c, up(v, n_vocab, step)), device_id_type=MESH)
    for step in range(1, n_dp):
        pl.semaphore_signal(barrier, inc=1, device_id=(up(g, n_dp, step), c, v), device_id_type=MESH)
    pl.semaphore_wait(barrier, n_ctx + n_vocab + n_dp - 3)

    own_cols = pl.ds(pl.multiple_of(v * quarter, quarter), quarter)
    pending = []
    z_copies = []
    for step in range(1, n_ctx):
        copy = remote(
            hid.at[:, own_cols], hbuf.at[own_rows, own_cols],
            z_send.at[step - 1], z_recv.at[step - 1], (g, up(c, n_ctx, step), v),
        )
        copy.start()
        z_copies.append(copy)
        pending.append(copy)

    seg = segments[...]
    token_adv = jnp.zeros((1, tokens), jnp.float32)
    token_len = jnp.zeros((1, tokens), jnp.float32)
    for s in range(advantages.shape[0]):
        here = seg == s
        token_adv = jnp.where(here, advantages[s], token_adv)
        token_len = jnp.where(here, lengths[s].astype(jnp.float32), token_len)
    token_weight = LOSS_SCALE * mask[...].astype(jnp.float32) / token_len
    rowbuf[...] = jnp.zeros_like(rowbuf)
    rowbuf[0:1, :] = targets[...].astype(jnp.float32)
    tcol[...] = rowbuf[...].T

    first_column = (c * n_vocab + v) * width
    columns = (first_column + lax.broadcasted_iota(jnp.int32, (block, width), 1)).astype(jnp.float32)
    lane = lax.broadcasted_iota(jnp.int32, (block, 128), 1)

    def do_block(owner):
        rows = pl.ds(pl.multiple_of(owner * block, block), block)
        x = jnp.dot(hbuf[rows, :], weight[...], preferred_element_type=jnp.float32)
        logits[rows, :] = x
        top = jnp.max(x, axis=1, keepdims=True)
        e = jnp.exp(x - top)
        total = jnp.sum(e, axis=1, keepdims=True)
        logit = jnp.sum(e * x, axis=1, keepdims=True)
        hit = tcol[rows, 0:1] == columns
        target = jnp.sum(jnp.where(hit, x, 0.0), axis=1, keepdims=True)
        statcol[rows, :] = jnp.where(
            lane == 0, top, jnp.where(lane == 1, total, jnp.where(lane == 2, logit, jnp.where(lane == 3, target, 0.0)))
        )

    load_w.wait()
    load_h.wait()
    do_block(c)

    x_copies = []
    for step in range(1, n_ctx):
        z_copies[step - 1].wait_recv()
        owner = down(c, n_ctx, step)
        rows = pl.ds(pl.multiple_of(owner * block, block), block)
        for hop in range(1, n_vocab):
            copy = remote(
                hbuf.at[rows, own_cols], hbuf.at[rows, own_cols],
                x_send.at[step - 1, hop - 1], x_recv.at[step - 1, hop - 1], (g, c, up(v, n_vocab, hop)),
            )
            copy.start()
            x_copies.append(copy)
    for step in range(1, n_ctx):
        for hop in range(1, n_vocab):
            x_copies[(step - 1) * (n_vocab - 1) + hop - 1].wait_recv()
        do_block(down(c, n_ctx, step))

    store_h = pltpu.make_async_copy(hbuf, hid_all.at[g], local_sem.at[2])
    store_h.start()
    d_copies = []
    for step in range(1, n_dp):
        copy = remote(hbuf, hid_all.at[g], d_send.at[step - 1], d_recv.at[step - 1], (up(g, n_dp, step), c, v))
        copy.start()
        d_copies.append(copy)

    stat_own[...] = statcol[...].T[0:STATS, :]
    s_copies = []
    for step in range(1, n_vocab):
        copy = remote(stat_own, stat_v.at[step - 1], sv_send.at[step - 1], sv_recv.at[step - 1], (g, c, up(v, n_vocab, step)))
        copy.start()
        s_copies.append(copy)
    for copy in s_copies:
        copy.wait_recv()
    pending += s_copies
    merged = combine([stat_own[...]] + [stat_v[i] for i in range(n_vocab - 1)])
    for i, row in enumerate(merged):
        stat_mid[i : i + 1, :] = row
    s_copies = []
    for step in range(1, n_ctx):
        copy = remote(stat_mid, stat_c.at[step - 1], sc_send.at[step - 1], sc_recv.at[step - 1], (g, up(c, n_ctx, step), v))
        copy.start()
        s_copies.append(copy)
    for copy in s_copies:
        copy.wait_recv()
    pending += s_copies
    row_max, exp_total, exp_logit, target_logit = combine([stat_mid[...]] + [stat_c[i] for i in range(n_ctx - 1)])
    log_total = row_max + jnp.log(exp_total)
    rowbuf[0:1, :] = log_total
    rowbuf[1:2, :] = exp_logit / exp_total
    rowbuf[2:3, :] = -token_adv + kl_weight * ((target_logit - log_total) - ref_lp[...])
    rowbuf[3:4, :] = token_weight
    colbuf[...] = rowbuf[...].T

    for b in range(n_ctx):
        rows = slice(b * block, (b + 1) * block)
        x = logits[rows, :]
        probs = jnp.exp(x - colbuf[rows, 0:1])
        hit = (tcol[rows, 0:1] == columns).astype(jnp.float32)
        inner = colbuf[rows, 2:3] * (hit - probs)
        inner = inner + entropy_weight * probs * (x - colbuf[rows, 1:2])
        gbuf[rows, :] = (colbuf[rows, 3:4] * inner).astype(jnp.bfloat16)

    store_g = pltpu.make_async_copy(gbuf, grad_all.at[g], local_sem.at[3])
    store_g.start()
    for step in range(1, n_dp):
        copy = remote(gbuf, grad_all.at[g], g_send.at[step - 1], g_recv.at[step - 1], (up(g, n_dp, step), c, v))
        copy.start()
        d_copies.append(copy)

    a_copies = []
    for k in range(CHUNKS):
        cols = slice(k * chunk, (k + 1) * chunk)
        part = lax.dot_general(
            gbuf[...], weight[cols, :], (((1,), (1,)), ((), ())), preferred_element_type=jnp.float32
        )
        for i in range(n_ctx):
            for j in range(n_vocab):
                first = i * block + j * out_rows
                pbuf[j, i, :, cols] = part[first : first + out_rows].astype(jnp.bfloat16)
        for step in range(1, n_vocab):
            to = up(v, n_vocab, step)
            copy = remote(
                pbuf.at[to, :, :, pl.ds(k * chunk, chunk)], part_v.at[step - 1, :, :, pl.ds(k * chunk, chunk)],
                a_send.at[k, step - 1], a_recv.at[k, step - 1], (g, c, to),
            )
            copy.start()
            a_copies.append(copy)
    b_copies = []
    for k in range(CHUNKS):
        cols = slice(k * chunk, (k + 1) * chunk)
        for step in range(1, n_vocab):
            a_copies[k * (n_vocab - 1) + step - 1].wait_recv()
        for i in range(n_ctx):
            total = pbuf[v, i, :, cols].astype(jnp.float32)
            for step in range(1, n_vocab):
                total = total + part_v[step - 1, i, :, cols].astype(jnp.float32)
            sums[i, :, cols] = total.astype(jnp.bfloat16)
        for step in range(1, n_ctx):
            to = up(c, n_ctx, step)
            copy = remote(
                sums.at[to, :, pl.ds(k * chunk, chunk)], part_c.at[step - 1, :, pl.ds(k * chunk, chunk)],
                b_send.at[k, step - 1], b_recv.at[k, step - 1], (g, to, v),
            )
            copy.start()
            b_copies.append(copy)
    for k in range(CHUNKS):
        cols = slice(k * chunk, (k + 1) * chunk)
        for step in range(1, n_ctx):
            b_copies[k * (n_ctx - 1) + step - 1].wait_recv()
        total = sums[c, :, cols].astype(jnp.float32)
        for step in range(1, n_ctx):
            total = total + part_c[step - 1, :, cols].astype(jnp.float32)
        rows_out[:, cols] = total.astype(jnp.bfloat16)

    for copy in pending + x_copies + a_copies + b_copies:
        copy.wait_send()
    for copy in d_copies:
        copy.wait()
    store_h.wait()
    store_g.wait()


def per_device(
    hidden, head_weight, targets, segment_ids, lengths, loss_mask, advantages, ref_logprobs
):
    n_dp, n_ctx, n_vocab = lax.axis_size("dp"), lax.axis_size("ctx"), lax.axis_size("vocab")
    block, depth = hidden.shape
    width = head_weight.shape[1]
    tokens = block * n_ctx
    out_rows = block // n_vocab
    bf16, f32 = jnp.bfloat16, jnp.float32
    dma = pltpu.SemaphoreType.DMA
    anywhere = pl.BlockSpec(memory_space=pl.ANY)
    smem = pl.BlockSpec(memory_space=pltpu.SMEM)
    vmem = pl.BlockSpec(memory_space=pltpu.VMEM)
    grad_hidden, hid_all, grad_all = pl.pallas_call(
        functools.partial(kernel, n_dp, n_ctx, n_vocab),
        out_shape=(
            jax.ShapeDtypeStruct((out_rows, depth), bf16),
            jax.ShapeDtypeStruct((n_dp, tokens, depth), bf16),
            jax.ShapeDtypeStruct((n_dp, tokens, width), bf16),
        ),
        in_specs=[anywhere, anywhere, smem, smem, vmem, vmem, vmem, vmem],
        out_specs=(vmem, anywhere, anywhere),
        scratch_shapes=[
            pltpu.VMEM((depth, width), bf16),
            pltpu.VMEM((tokens, depth), bf16),
            pltpu.VMEM((tokens, width), f32),
            pltpu.VMEM((128, tokens), f32),
            pltpu.VMEM((tokens, 128), f32),
            pltpu.VMEM((tokens, 128), f32),
            pltpu.VMEM((tokens, 128), f32),
            pltpu.VMEM((STATS, tokens), f32),
            pltpu.VMEM((STATS, tokens), f32),
            pltpu.VMEM((n_vocab - 1, STATS, tokens), f32),
            pltpu.VMEM((n_ctx - 1, STATS, tokens), f32),
            pltpu.VMEM((tokens, width), bf16),
            pltpu.VMEM((n_vocab, n_ctx, out_rows, depth), bf16),
            pltpu.VMEM((n_vocab - 1, n_ctx, out_rows, depth), bf16),
            pltpu.VMEM((n_ctx, out_rows, depth), bf16),
            pltpu.VMEM((n_ctx - 1, out_rows, depth), bf16),
            dma((4,)),
            dma((n_ctx - 1,)), dma((n_ctx - 1,)),
            dma((n_ctx - 1, n_vocab - 1)), dma((n_ctx - 1, n_vocab - 1)),
            dma((n_dp - 1,)), dma((n_dp - 1,)), dma((n_dp - 1,)), dma((n_dp - 1,)),
            dma((n_vocab - 1,)), dma((n_vocab - 1,)),
            dma((n_ctx - 1,)), dma((n_ctx - 1,)),
            dma((CHUNKS, n_vocab - 1)), dma((CHUNKS, n_vocab - 1)),
            dma((CHUNKS, n_ctx - 1)), dma((CHUNKS, n_ctx - 1)),
        ],
        compiler_params=pltpu.CompilerParams(collective_id=0, has_side_effects=True),
    )(
        hidden, head_weight, lengths, advantages,
        targets[None, :], segment_ids[None, :], loss_mask[None, :], ref_logprobs[None, :],
    )
    grad_head = lax.dot_general(
        hid_all.reshape(n_dp * tokens, depth),
        grad_all.reshape(n_dp * tokens, width),
        (((0,), (0,)), ((), ())),
        preferred_element_type=jnp.float32,
    ).astype(jnp.bfloat16)
    return (grad_hidden, grad_head)


def solution(mesh):
    return jax.shard_map(
        per_device,
        mesh=mesh,
        in_specs=(
            P(("dp", "ctx"), None),
            P(None, ("ctx", "vocab")),
            P("dp"),
            P("dp"),
            P(),
            P("dp"),
            P(),
            P("dp"),
        ),
        out_specs=(P(("dp", "ctx", "vocab"), None), P(None, ("ctx", "vocab"))),
        check_vma=False,
    )
```

time: 282 us -> 83.4 us (0.30)
  waiting for transfers between devices: 167 us -> 0 us
  blocking collectives: 76.1 us -> 0 us
  Pallas kernels: 0 us -> 66.7 us
  between operations: 13.8 us -> 0.65 us
  matrix products: 14.9 us -> 7.39 us
  other arithmetic: 3.95 us -> 0 us
    reduce_scatter x1 -> x0, waiting for transfers between devices: 87.7 us -> none  [per_device(): lax.psum_scatter(lax.dot_general(grad_logits, head_weight, (((1,), (1,)),...]
    pallas_call x0 -> x1, Pallas kernels: none -> 66.7 us  [per_device(): pl.pallas_call(functools.partial(kernel, n_dp, n_ctx, n_vocab), out_shape...]
    all_gather x1 -> x0, waiting for transfers between devices: 47.9 us -> none  [per_device(): gathered = lax.all_gather(hidden, 'ctx', axis=0, tiled=True)]
    pmax x1 -> x0, blocking collectives: 39.5 us -> none  [per_device(): row_max = lax.pmax(jnp.max(logits, axis=1), ('ctx', 'vocab'))]
    psum x1 -> x0, blocking collectives: 36.6 us -> none  [per_device(): lax.psum((jnp.sum(shifted, axis=1), jnp.sum(shifted * logits, axis=1), ta...]
    psum x1 -> x0, waiting for transfers between devices: 30.2 us -> none  [per_device(): lax.psum(head_local, 'dp').astype(jnp.float32).astype(jnp.bfloat16)]
    dot_general x3 -> x1, matrix products: 14.9 us -> 7.39 us  [per_device(): lax.dot_general(hid_all.reshape(n_dp * tokens, depth), grad_all.reshape(n...]
    unnamed x7 -> x4, local copies, waits for them, and re-layouts: 6.77 us -> 8.42 us
  transfers between devices with their start and end apart: 3 -> 0, of which waited for: 3 -> 0; matrix products, arithmetic and copies ran while one was open for 3% -> 0% of each run, Pallas kernels for 0% -> 0%
where the time goes in v1:
time: 83.4 us; the launch traced here: 83.1 us
  Pallas kernels  66.7 us (80%)
  local copies, waits for them, and re-layouts  8.42 us (10%)
  matrix products  7.39 us (9%)
    pallas_call x1, Pallas kernels, per_device(): pl.pallas_call(functools.partial(kernel, n_dp, n_ctx, n_vocab), out_shape...  66.7 us
    unnamed x4, local copies, waits for them, and re-layouts  8.42 us
    dot_general x1, matrix products, per_device(): lax.dot_general(hid_all.reshape(n_dp * tokens, depth), grad_all.reshape(n...  7.39 us

profile of v1, /device:TPU:0, one launch (start us, length us, event | category | flops | bytes accessed | tf_op | source)
XLA Modules:
  0.0 83.1 jit_solution(16978280879104930584)
XLA Ops:
  0.6 7.8 %copy.10.head = bf16[4096,594]{1,0:T(8,128)(2,1)} copy(bf16[4096,594]{0,1:T(8,128)(2,1)} %param.9) | data formatting | bytes 9732096 | tf_op args[1]
  8.4 66.7 %shard_map.95 = (bf16[16,4096]{1,0:T(8,128)(2,1)}, bf16[2,256,4096]{2,1,0:T(8,128)(2,1)}, bf16[2,256,594]{2,1,0:T(8,128)(2,1)}) custom-call(bf16[64,4096]{1,0:T(8,128)(2,1)} %hid.1, bf16[4096,594]{1,0:T(8,128)(2,1)} %copy.10.head, s32[32]{0:T(128)} %lengths.1, f32[32]{0:T(128)} %advantages.1, s32[1,256]{1,0:T(1,128)} %bitcast.8, s32[1,256]{1,0:T(1,128)} %bitcast.9, ...), custom_call_target="tpu_custom_call" | custom-call | tf_op jit(solution)/shard_map/pallas_call | solution.py:254
  75.1 0.0 copy-start
  75.1 7.4 %bitcast_convert_fusion = bf16[4096,594]{0,1:T(8,128)(2,1)} fusion(bf16[2,256,4096]{2,1,0:T(8,128)(2,1)} %get-tuple-element.6, bf16[2,256,594]{2,1,0:T(8,128)(2,1)} %get-tuple-element.7), kind=kOutput, calls=%fused_computation | convolution fusion | flops 2493849600 | bytes 9668608 | tf_op jit(solution)/shard_map/dot_general | solution.py:294
  82.5 0.0 copy-done
  82.5 0.7 copy.14
Async XLA Ops:
  75.1 7.4 %copy-start = (bf16[16,4096]{1,0:T(8,128)(2,1)S(1)}, bf16[16,4096]{1,0:T(8,128)(2,1)}, u32[]{:S(2)}) copy-start(bf16[16,4096]{1,0:T(8,128)(2,1)} %get-tuple-element.10) | copy-start | bytes 393220

commit v2 on v1

--- a/solution.py
+++ b/solution.py
@@ -1,4 +1,5 @@
 import functools
+import math
 
 import jax
 import jax.numpy as jnp
@@ -13,7 +14,7 @@
 kl_weight = 0.1
 entropy_weight = 0.05
 MESH = pl.DeviceIdType.MESH
-CHUNKS = 4
+CHUNKS = 8
 STATS = 8
 
 
@@ -27,15 +28,18 @@
 
 
 def kernel(
-    n_dp, n_ctx, n_vocab,
+    n_dp, n_ctx, n_hi, n_lo,
     hid, head, lengths, advantages, targets, segments, mask, ref_lp,
     rows_out, hid_all, grad_all,
     weight, hbuf, logits, rowbuf, colbuf, tcol, statcol, stat_own, stat_mid, stat_v, stat_c,
-    gbuf, pbuf, part_v, sums, part_c,
-    local_sem, z_send, z_recv, x_send, x_recv, d_send, d_recv, g_send, g_recv,
-    sv_send, sv_recv, sc_send, sc_recv, a_send, a_recv, b_send, b_recv,
+    gbuf, pbuf, part_one, sum_one, part_two, sums, part_c,
+    local_sem, z_send, z_recv, lo_send, lo_recv, hi_send, hi_recv, ra_send, ra_recv, rb_send, rb_recv,
+    d_send, d_recv, g_send, g_recv,
+    sv_send, sv_recv, sc_send, sc_recv, one_send, one_recv, two_send, two_recv, b_send, b_recv,
 ):
     g, c, v = lax.axis_index("dp"), lax.axis_index("ctx"), lax.axis_index("vocab")
+    n_vocab = n_hi * n_lo
+    hi, lo = v // n_lo, lax.rem(v, n_lo)
     block, depth = hid.shape
     tokens, width = logits.shape
     quarter = depth // n_vocab
@@ -100,7 +104,9 @@
 
     def do_block(owner):
         rows = pl.ds(pl.multiple_of(owner * block, block), block)
-        x = jnp.dot(hbuf[rows, :], weight[...], preferred_element_type=jnp.float32)
+        x = lax.dot_general(
+            weight[...], hbuf[rows, :], (((1,), (1,)), ((), ())), preferred_element_type=jnp.float32
+        ).T
         logits[rows, :] = x
         top = jnp.max(x, axis=1, keepdims=True)
         e = jnp.exp(x - top)
@@ -116,21 +122,62 @@
     load_h.wait()
     do_block(c)
 
-    x_copies = []
+    half = quarter // 2
+
+    def share(owner, column_owner, part):
+        rows = pl.ds(pl.multiple_of(owner * block, block), block)
+        return hbuf.at[rows, pl.ds(pl.multiple_of(column_owner * quarter + part * half, half), half)]
+
+    def at_lo(step):
+        return (g, c, hi * n_lo + up(lo, n_lo, step))
+
+    def at_hi(step):
+        return (g, c, up(hi, n_hi, step) * n_lo + lo)
+
+    def move(ref, send, recv, where):
+        copy = remote(ref, ref, send, recv, where)
+        copy.start()
+        pending.append(copy)
+        return copy
+
+    lo_copies, hi_copies, relays = {}, {}, {}
+
+    def relay(step):
+        owner = down(c, n_ctx, step)
+        for hop in range(1, n_lo):
+            lo_copies[step - 1, hop - 1, 0].wait_recv()
+            source = hi * n_lo + down(lo, n_lo, hop)
+            for far in range(1, n_hi):
+                at = (step - 1, hop - 1, far - 1)
+                relays[(step, 0) + at] = move(share(owner, source, 0), ra_send.at[at], ra_recv.at[at], at_hi(far))
+        for hop in range(1, n_hi):
+            hi_copies[step - 1, hop - 1, 1].wait_recv()
+            source = down(hi, n_hi, hop) * n_lo + lo
+            for far in range(1, n_lo):
+                at = (step - 1, hop - 1, far - 1)
+                relays[(step, 1) + at] = move(share(owner, source, 1), rb_send.at[at], rb_recv.at[at], at_lo(far))
+
     for step in range(1, n_ctx):
         z_copies[step - 1].wait_recv()
         owner = down(c, n_ctx, step)
-        rows = pl.ds(pl.multiple_of(owner * block, block), block)
-        for hop in range(1, n_vocab):
-            copy = remote(
-                hbuf.at[rows, own_cols], hbuf.at[rows, own_cols],
-                x_send.at[step - 1, hop - 1], x_recv.at[step - 1, hop - 1], (g, c, up(v, n_vocab, hop)),
-            )
-            copy.start()
-            x_copies.append(copy)
+        for part in range(2):
+            for hop in range(1, n_lo):
+                at = (step - 1, hop - 1, part)
+                lo_copies[at] = move(share(owner, v, part), lo_send.at[at], lo_recv.at[at], at_lo(hop))
+            for hop in range(1, n_hi):
+                at = (step - 1, hop - 1, 1 - part)
+                hi_copies[at] = move(share(owner, v, 1 - part), hi_send.at[at], hi_recv.at[at], at_hi(hop))
+        if step >= 2:
+            relay(step - 1)
+    relay(n_ctx - 1)
     for step in range(1, n_ctx):
-        for hop in range(1, n_vocab):
-            x_copies[(step - 1) * (n_vocab - 1) + hop - 1].wait_recv()
+        for copies in (lo_copies, hi_copies):
+            for at, copy in copies.items():
+                if at[0] == step - 1 and at[2] == (1 if copies is lo_copies else 0):
+                    copy.wait_recv()
+        for at, copy in relays.items():
+            if at[0] == step:
+                copy.wait_recv()
         do_block(down(c, n_ctx, step))
 
     store_h = pltpu.make_async_copy(hbuf, hid_all.at[g], local_sem.at[2])
@@ -185,42 +232,85 @@
         copy.start()
         d_copies.append(copy)
 
-    a_copies = []
-    for k in range(CHUNKS):
-        cols = slice(k * chunk, (k + 1) * chunk)
-        part = lax.dot_general(
-            gbuf[...], weight[cols, :], (((1,), (1,)), ((), ())), preferred_element_type=jnp.float32
-        )
+    def span(k):
+        return pl.ds(k * chunk, chunk)
+
+    def partials(k):
+        part = jnp.dot(gbuf[...], weight[:, k * chunk : (k + 1) * chunk], preferred_element_type=jnp.float32)
         for i in range(n_ctx):
             for j in range(n_vocab):
                 first = i * block + j * out_rows
-                pbuf[j, i, :, cols] = part[first : first + out_rows].astype(jnp.bfloat16)
-        for step in range(1, n_vocab):
-            to = up(v, n_vocab, step)
+                pbuf[j // n_lo, j % n_lo, i, :, span(k)] = part[first : first + out_rows].astype(jnp.bfloat16)
+
+    def stage_one(k):
+        copies = []
+        for step in range(1, n_hi if k % 2 else n_lo):
+            if k % 2:
+                source = pbuf.at[up(hi, n_hi, step), :, :, :, span(k)]
+            else:
+                source = pbuf.at[:, up(lo, n_lo, step), :, :, span(k)]
             copy = remote(
-                pbuf.at[to, :, :, pl.ds(k * chunk, chunk)], part_v.at[step - 1, :, :, pl.ds(k * chunk, chunk)],
-                a_send.at[k, step - 1], a_recv.at[k, step - 1], (g, c, to),
+                source, part_one.at[step - 1, pl.ds(0, source.shape[0]), :, :, span(k)],
+                one_send.at[k, step - 1], one_recv.at[k, step - 1], at_hi(step) if k % 2 else at_lo(step),
             )
             copy.start()
-            a_copies.append(copy)
-    b_copies = []
-    for k in range(CHUNKS):
-        cols = slice(k * chunk, (k + 1) * chunk)
-        for step in range(1, n_vocab):
-            a_copies[k * (n_vocab - 1) + step - 1].wait_recv()
-        for i in range(n_ctx):
-            total = pbuf[v, i, :, cols].astype(jnp.float32)
-            for step in range(1, n_vocab):
-                total = total + part_v[step - 1, i, :, cols].astype(jnp.float32)
-            sums[i, :, cols] = total.astype(jnp.bfloat16)
+            copies.append(copy)
+        return copies
+
+    def stage_two(k, copies):
+        for copy in copies:
+            copy.wait_recv()
+        for i in range(n_lo if k % 2 else n_hi):
+            own = pbuf[hi, i, :, :, span(k)] if k % 2 else pbuf[i, lo, :, :, span(k)]
+            total = own.astype(jnp.float32)
+            for j in range(len(copies)):
+                total = total + part_one[j, i, :, :, span(k)].astype(jnp.float32)
+            sum_one[i, :, :, span(k)] = total.astype(jnp.bfloat16)
+        started = []
+        for step in range(1, n_lo if k % 2 else n_hi):
+            to = up(lo, n_lo, step) if k % 2 else up(hi, n_hi, step)
+            copy = remote(
+                sum_one.at[to, :, :, span(k)], part_two.at[step - 1, :, :, span(k)],
+                two_send.at[k, step - 1], two_recv.at[k, step - 1], at_lo(step) if k % 2 else at_hi(step),
+            )
+            copy.start()
+            started.append(copy)
+        return started
+
+    def stage_three(k, copies):
+        for copy in copies:
+            copy.wait_recv()
+        total = sum_one[lo if k % 2 else hi, :, :, span(k)].astype(jnp.float32)
+        for j in range(len(copies)):
+            total = total + part_two[j, :, :, span(k)].astype(jnp.float32)
+        sums[:, :, span(k)] = total.astype(jnp.bfloat16)
+        started = []
         for step in range(1, n_ctx):
             to = up(c, n_ctx, step)
             copy = remote(
-                sums.at[to, :, pl.ds(k * chunk, chunk)], part_c.at[step - 1, :, pl.ds(k * chunk, chunk)],
+                sums.at[to, :, span(k)], part_c.at[step - 1, :, span(k)],
                 b_send.at[k, step - 1], b_recv.at[k, step - 1], (g, to, v),
             )
             copy.start()
-            b_copies.append(copy)
+            started.append(copy)
+        return started
+
+    one, two, b_copies = {}, {}, []
+    for k in range(CHUNKS):
+        partials(k)
+        if k < 4:
+            one[k] = stage_one(k)
+    for p in range(0, CHUNKS + 2, 2):
+        for k in (p, p + 1):
+            if k < CHUNKS:
+                two[k] = stage_two(k, one[k])
+                if k + 4 < CHUNKS:
+                    one[k + 4] = stage_one(k + 4)
+        for k in (p - 2, p - 1):
+            if k >= 0:
+                b_copies += stage_three(k, two[k])
+    for copies in list(one.values()) + list(two.values()):
+        pending += copies
     for k in range(CHUNKS):
         cols = slice(k * chunk, (k + 1) * chunk)
         for step in range(1, n_ctx):
@@ -230,7 +320,7 @@
             total = total + part_c[step - 1, :, cols].astype(jnp.float32)
         rows_out[:, cols] = total.astype(jnp.bfloat16)
 
-    for copy in pending + x_copies + a_copies + b_copies:
+    for copy in pending + b_copies:
         copy.wait_send()
     for copy in d_copies:
         copy.wait()
@@ -244,6 +334,10 @@
     n_dp, n_ctx, n_vocab = lax.axis_size("dp"), lax.axis_size("ctx"), lax.axis_size("vocab")
     block, depth = hidden.shape
     width = head_weight.shape[1]
+    root = math.isqrt(n_vocab)
+    n_lo = root if root * root == n_vocab else n_vocab
+    n_hi = n_vocab // n_lo
+    wide = max(n_hi, n_lo)
     tokens = block * n_ctx
     out_rows = block // n_vocab
     bf16, f32 = jnp.bfloat16, jnp.float32
@@ -252,7 +346,7 @@
     smem = pl.BlockSpec(memory_space=pltpu.SMEM)
     vmem = pl.BlockSpec(memory_space=pltpu.VMEM)
     grad_hidden, hid_all, grad_all = pl.pallas_call(
-        functools.partial(kernel, n_dp, n_ctx, n_vocab),
+        functools.partial(kernel, n_dp, n_ctx, n_hi, n_lo),
         out_shape=(
             jax.ShapeDtypeStruct((out_rows, depth), bf16),
             jax.ShapeDtypeStruct((n_dp, tokens, depth), bf16),
@@ -261,7 +355,7 @@
         in_specs=[anywhere, anywhere, smem, smem, vmem, vmem, vmem, vmem],
         out_specs=(vmem, anywhere, anywhere),
         scratch_shapes=[
-            pltpu.VMEM((depth, width), bf16),
+            pltpu.VMEM((width, depth), bf16),
             pltpu.VMEM((tokens, depth), bf16),
             pltpu.VMEM((tokens, width), f32),
             pltpu.VMEM((128, tokens), f32),
@@ -273,30 +367,36 @@
             pltpu.VMEM((n_vocab - 1, STATS, tokens), f32),
             pltpu.VMEM((n_ctx - 1, STATS, tokens), f32),
             pltpu.VMEM((tokens, width), bf16),
-            pltpu.VMEM((n_vocab, n_ctx, out_rows, depth), bf16),
-            pltpu.VMEM((n_vocab - 1, n_ctx, out_rows, depth), bf16),
+            pltpu.VMEM((n_hi, n_lo, n_ctx, out_rows, depth), bf16),
+            pltpu.VMEM((wide - 1, wide, n_ctx, out_rows, depth), bf16),
+            pltpu.VMEM((wide, n_ctx, out_rows, depth), bf16),
+            pltpu.VMEM((wide - 1, n_ctx, out_rows, depth), bf16),
             pltpu.VMEM((n_ctx, out_rows, depth), bf16),
             pltpu.VMEM((n_ctx - 1, out_rows, depth), bf16),
             dma((4,)),
             dma((n_ctx - 1,)), dma((n_ctx - 1,)),
-            dma((n_ctx - 1, n_vocab - 1)), dma((n_ctx - 1, n_vocab - 1)),
+            dma((n_ctx - 1, wide, 2)), dma((n_ctx - 1, wide, 2)),
+            dma((n_ctx - 1, wide, 2)), dma((n_ctx - 1, wide, 2)),
+            dma((n_ctx - 1, wide, wide)), dma((n_ctx - 1, wide, wide)),
+            dma((n_ctx - 1, wide, wide)), dma((n_ctx - 1, wide, wide)),
             dma((n_dp - 1,)), dma((n_dp - 1,)), dma((n_dp - 1,)), dma((n_dp - 1,)),
             dma((n_vocab - 1,)), dma((n_vocab - 1,)),
             dma((n_ctx - 1,)), dma((n_ctx - 1,)),
-            dma((CHUNKS, n_vocab - 1)), dma((CHUNKS, n_vocab - 1)),
+            dma((CHUNKS, wide)), dma((CHUNKS, wide)),
+            dma((CHUNKS, wide)), dma((CHUNKS, wide)),
             dma((CHUNKS, n_ctx - 1)), dma((CHUNKS, n_ctx - 1)),
         ],
         compiler_params=pltpu.CompilerParams(collective_id=0, has_side_effects=True),
     )(
-        hidden, head_weight, lengths, advantages,
+        hidden, head_weight.T, lengths, advantages,
         targets[None, :], segment_ids[None, :], loss_mask[None, :], ref_logprobs[None, :],
     )
     grad_head = lax.dot_general(
+        grad_all.reshape(n_dp * tokens, width),
         hid_all.reshape(n_dp * tokens, depth),
-        grad_all.reshape(n_dp * tokens, width),
         (((0,), (0,)), ((), ())),
         preferred_element_type=jnp.float32,
-    ).astype(jnp.bfloat16)
+    ).astype(bf16).T
     return (grad_hidden, grad_head)
 
 

time: 83.4 us -> 75.1 us (0.900)
  local copies, waits for them, and re-layouts: 8.42 us -> 0.66 us
    unnamed x4 -> x3, local copies, waits for them, and re-layouts: 8.42 us -> 0.66 us
where the time goes in v2:
time: 75.1 us; the launch traced here: 75 us
  Pallas kernels  66.3 us (88%)
  matrix products  7.39 us (10%)
    pallas_call x1, Pallas kernels, per_device(): pl.pallas_call(functools.partial(kernel, n_dp, n_ctx, n_hi, n_lo), out_sh...  66.3 us
    dot_general x1, matrix products, per_device(): lax.dot_general(grad_all.reshape(n_dp * tokens, width), hid_all.reshape(n...  7.39 us

profile of v2, /device:TPU:0, one launch (start us, length us, event | category | flops | bytes accessed | tf_op | source)
XLA Modules:
  0.0 75.0 jit_solution(9739343847917031787)
XLA Ops:
  0.6 66.3 %shard_map.95 = (bf16[16,4096]{1,0:T(8,128)(2,1)}, bf16[2,256,4096]{2,1,0:T(8,128)(2,1)}, bf16[2,256,594]{2,1,0:T(8,128)(2,1)}) custom-call(bf16[64,4096]{1,0:T(8,128)(2,1)} %hid.1, bf16[594,4096]{1,0:T(8,128)(2,1)} %bitcast.9, s32[32]{0:T(128)} %lengths.1, f32[32]{0:T(128)} %advantages.1, s32[1,256]{1,0:T(1,128)} %bitcast.10, s32[1,256]{1,0:T(1,128)} %bitcast.11, ...), custom_call_target="tpu_custom_call" | custom-call | tf_op jit(solution)/shard_map/pallas_call | solution.py:348
  66.9 0.0 copy-start
  66.9 7.4 %bitcast_convert_fusion = bf16[4096,594]{0,1:T(8,128)(2,1)} fusion(bf16[2,256,4096]{2,1,0:T(8,128)(2,1)} %get-tuple-element.6, bf16[2,256,594]{2,1,0:T(8,128)(2,1)} %get-tuple-element.7), kind=kOutput, calls=%fused_computation | convolution fusion | flops 2493849600 | bytes 9668608 | tf_op jit(solution)/shard_map/dot_general | solution.py:394
  74.3 0.0 copy-done
  74.3 0.7 copy.13
Async XLA Ops:
  66.9 7.4 %copy-start = (bf16[16,4096]{1,0:T(8,128)(2,1)S(1)}, bf16[16,4096]{1,0:T(8,128)(2,1)}, u32[]{:S(2)}) copy-start(bf16[16,4096]{1,0:T(8,128)(2,1)} %get-tuple-element.10) | copy-start | bytes 393220

commit v3 on v2

--- a/solution.py
+++ b/solution.py
@@ -30,10 +30,10 @@
 def kernel(
     n_dp, n_ctx, n_hi, n_lo,
     hid, head, lengths, advantages, targets, segments, mask, ref_lp,
-    rows_out, hid_all, grad_all,
+    rows_out, head_out,
     weight, hbuf, logits, rowbuf, colbuf, tcol, statcol, stat_own, stat_mid, stat_v, stat_c,
-    gbuf, pbuf, part_one, sum_one, part_two, sums, part_c,
-    local_sem, z_send, z_recv, lo_send, lo_recv, hi_send, hi_recv, ra_send, ra_recv, rb_send, rb_recv,
+    hid_other, g_own, g_other, head_buf, gbuf, pbuf, part_one, sum_one, part_two, sums, part_c,
+    local_sem, head_sem, z_send, z_recv, lo_send, lo_recv, hi_send, hi_recv, ra_send, ra_recv, rb_send, rb_recv,
     d_send, d_recv, g_send, g_recv,
     sv_send, sv_recv, sc_send, sc_recv, one_send, one_recv, two_send, two_recv, b_send, b_recv,
 ):
@@ -180,11 +180,9 @@
                 copy.wait_recv()
         do_block(down(c, n_ctx, step))
 
-    store_h = pltpu.make_async_copy(hbuf, hid_all.at[g], local_sem.at[2])
-    store_h.start()
     d_copies = []
     for step in range(1, n_dp):
-        copy = remote(hbuf, hid_all.at[g], d_send.at[step - 1], d_recv.at[step - 1], (up(g, n_dp, step), c, v))
+        copy = remote(hbuf, hid_other.at[step - 1], d_send.at[step - 1], d_recv.at[step - 1], (up(g, n_dp, step), c, v))
         copy.start()
         d_copies.append(copy)
 
@@ -224,13 +222,6 @@
         inner = colbuf[rows, 2:3] * (hit - probs)
         inner = inner + entropy_weight * probs * (x - colbuf[rows, 1:2])
         gbuf[rows, :] = (colbuf[rows, 3:4] * inner).astype(jnp.bfloat16)
-
-    store_g = pltpu.make_async_copy(gbuf, grad_all.at[g], local_sem.at[3])
-    store_g.start()
-    for step in range(1, n_dp):
-        copy = remote(gbuf, grad_all.at[g], g_send.at[step - 1], g_recv.at[step - 1], (up(g, n_dp, step), c, v))
-        copy.start()
-        d_copies.append(copy)
 
     def span(k):
         return pl.ds(k * chunk, chunk)
@@ -300,7 +291,30 @@
         partials(k)
         if k < 4:
             one[k] = stage_one(k)
+    g_own[...] = gbuf[...].astype(jnp.float32).T.astype(jnp.bfloat16)
+    g_copies = []
+    for step in range(1, n_dp):
+        copy = remote(g_own, g_other.at[step - 1], g_send.at[step - 1], g_recv.at[step - 1], (up(g, n_dp, step), c, v))
+        copy.start()
+        g_copies.append(copy)
+
+    def head_chunk(k):
+        cols = slice(k * chunk, (k + 1) * chunk)
+        total = jnp.dot(g_own[...], hbuf[:, cols], preferred_element_type=jnp.float32)
+        for i in range(n_dp - 1):
+            total = total + jnp.dot(g_other[i], hid_other[i, :, cols], preferred_element_type=jnp.float32)
+        head_buf[:, cols] = total.astype(jnp.bfloat16)
+        copy = pltpu.make_async_copy(head_buf.at[:, span(k)], head_out.at[:, span(k)], head_sem.at[k])
+        copy.start()
+        return copy
+
+    stores = []
     for p in range(0, CHUNKS + 2, 2):
+        if p == 2:
+            for copy in d_copies + g_copies:
+                copy.wait_recv()
+        if p >= 2:
+            stores += [head_chunk(p - 2), head_chunk(p - 1)]
         for k in (p, p + 1):
             if k < CHUNKS:
                 two[k] = stage_two(k, one[k])
@@ -322,10 +336,10 @@
 
     for copy in pending + b_copies:
         copy.wait_send()
-    for copy in d_copies:
+    for copy in d_copies + g_copies:
+        copy.wait_send()
+    for copy in stores:
         copy.wait()
-    store_h.wait()
-    store_g.wait()
 
 
 def per_device(
@@ -345,15 +359,14 @@
     anywhere = pl.BlockSpec(memory_space=pl.ANY)
     smem = pl.BlockSpec(memory_space=pltpu.SMEM)
     vmem = pl.BlockSpec(memory_space=pltpu.VMEM)
-    grad_hidden, hid_all, grad_all = pl.pallas_call(
+    grad_hidden, grad_head = pl.pallas_call(
         functools.partial(kernel, n_dp, n_ctx, n_hi, n_lo),
         out_shape=(
             jax.ShapeDtypeStruct((out_rows, depth), bf16),
-            jax.ShapeDtypeStruct((n_dp, tokens, depth), bf16),
-            jax.ShapeDtypeStruct((n_dp, tokens, width), bf16),
+            jax.ShapeDtypeStruct((width, depth), bf16),
         ),
         in_specs=[anywhere, anywhere, smem, smem, vmem, vmem, vmem, vmem],
-        out_specs=(vmem, anywhere, anywhere),
+        out_specs=(vmem, anywhere),
         scratch_shapes=[
             pltpu.VMEM((width, depth), bf16),
             pltpu.VMEM((tokens, depth), bf16),
@@ -366,6 +379,10 @@
             pltpu.VMEM((STATS, tokens), f32),
             pltpu.VMEM((n_vocab - 1, STATS, tokens), f32),
             pltpu.VMEM((n_ctx - 1, STATS, tokens), f32),
+            pltpu.VMEM((n_dp - 1, tokens, depth), bf16),
+            pltpu.VMEM((width, tokens), bf16),
+            pltpu.VMEM((n_dp - 1, width, tokens), bf16),
+            pltpu.VMEM((width, depth), bf16),
             pltpu.VMEM((tokens, width), bf16),
             pltpu.VMEM((n_hi, n_lo, n_ctx, out_rows, depth), bf16),
             pltpu.VMEM((wide - 1, wide, n_ctx, out_rows, depth), bf16),
@@ -373,7 +390,7 @@
             pltpu.VMEM((wide - 1, n_ctx, out_rows, depth), bf16),
             pltpu.VMEM((n_ctx, out_rows, depth), bf16),
             pltpu.VMEM((n_ctx - 1, out_rows, depth), bf16),
-            dma((4,)),
+            dma((2,)), dma((CHUNKS,)),
             dma((n_ctx - 1,)), dma((n_ctx - 1,)),
             dma((n_ctx - 1, wide, 2)), dma((n_ctx - 1, wide, 2)),
             dma((n_ctx - 1, wide, 2)), dma((n_ctx - 1, wide, 2)),
@@ -391,13 +408,7 @@
         hidden, head_weight.T, lengths, advantages,
         targets[None, :], segment_ids[None, :], loss_mask[None, :], ref_logprobs[None, :],
     )
-    grad_head = lax.dot_general(
-        grad_all.reshape(n_dp * tokens, width),
-        hid_all.reshape(n_dp * tokens, depth),
-        (((0,), (0,)), ((), ())),
-        preferred_element_type=jnp.float32,
-    ).astype(bf16).T
-    return (grad_hidden, grad_head)
+    return (grad_hidden, grad_head.T)
 
 
 def solution(mesh):

time: 75.1 us -> 75.2 us (level)
  matrix products: 7.39 us -> 0 us
  local copies, waits for them, and re-layouts: 0.66 us -> 6.81 us
  Pallas kernels: 66.3 us -> 67.5 us
    dot_general x1 -> x0, matrix products: 7.39 us -> none  [per_device(): lax.dot_general(grad_all.reshape(n_dp * tokens, width), hid_all.reshape(n...]
    unnamed x3 -> x2, local copies, waits for them, and re-layouts: 0.66 us -> 6.81 us
    pallas_call x1, Pallas kernels: 66.3 us -> 67.5 us  [per_device(): pl.pallas_call(functools.partial(kernel, n_dp, n_ctx, n_hi, n_lo), out_sh...]
where the time goes in v3:
time: 75.2 us; the launch traced here: 75 us
  Pallas kernels  67.5 us (90%)
  local copies, waits for them, and re-layouts  6.81 us (9%)
    pallas_call x1, Pallas kernels, per_device(): pl.pallas_call(functools.partial(kernel, n_dp, n_ctx, n_hi, n_lo), out_sh...  67.5 us
    unnamed x2, local copies, waits for them, and re-layouts  6.81 us

profile of v3, /device:TPU:0, one launch (start us, length us, event | category | flops | bytes accessed | tf_op | source)
XLA Modules:
  0.0 75.0 jit_solution(10045561542767507300)
XLA Ops:
  0.6 67.5 %shard_map.95 = (bf16[16,4096]{1,0:T(8,128)(2,1)}, bf16[594,4096]{1,0:T(8,128)(2,1)}) custom-call(bf16[64,4096]{1,0:T(8,128)(2,1)} %hid.1, bf16[594,4096]{1,0:T(8,128)(2,1)} %bitcast.6, s32[32]{0:T(128)} %lengths.1, f32[32]{0:T(128)} %advantages.1, s32[1,256]{1,0:T(1,128)} %bitcast.8, s32[1,256]{1,0:T(1,128)} %bitcast.9, s32[1,256]{1,0:T(1,128)} %bitcast.10, ...), custom_call_target="tpu_custom_call" | custom-call | tf_op jit(solution)/shard_map/pallas_call | solution.py:362
  68.2 1.6 %copy.12 = bf16[16,4096]{1,0:T(8,128)(2,1)} copy(bf16[16,4096]{1,0:T(8,128)(2,1)} %get-tuple-element.8) | data formatting | bytes 262144
  69.8 5.2 %copy.13 = bf16[4096,594]{0,1:T(8,128)(2,1)} copy(bf16[4096,594]{0,1:T(8,128)(2,1)} %bitcast.7) | data formatting | bytes 9732096

commit v4 on v2

--- a/solution.py
+++ b/solution.py
@@ -74,17 +74,18 @@
         pl.semaphore_signal(barrier, inc=1, device_id=(up(g, n_dp, step), c, v), device_id_type=MESH)
     pl.semaphore_wait(barrier, n_ctx + n_vocab + n_dp - 3)
 
-    own_cols = pl.ds(pl.multiple_of(v * quarter, quarter), quarter)
     pending = []
-    z_copies = []
+    z_copies = {}
     for step in range(1, n_ctx):
-        copy = remote(
-            hid.at[:, own_cols], hbuf.at[own_rows, own_cols],
-            z_send.at[step - 1], z_recv.at[step - 1], (g, up(c, n_ctx, step), v),
-        )
-        copy.start()
-        z_copies.append(copy)
-        pending.append(copy)
+        for part in range(2):
+            cols = pl.ds(pl.multiple_of(v * quarter + part * (quarter // 2), quarter // 2), quarter // 2)
+            copy = remote(
+                hid.at[:, cols], hbuf.at[own_rows, cols],
+                z_send.at[step - 1, part], z_recv.at[step - 1, part], (g, up(c, n_ctx, step), v),
+            )
+            copy.start()
+            z_copies[step - 1, part] = copy
+            pending.append(copy)
 
     seg = segments[...]
     token_adv = jnp.zeros((1, tokens), jnp.float32)
@@ -157,20 +158,7 @@
                 at = (step - 1, hop - 1, far - 1)
                 relays[(step, 1) + at] = move(share(owner, source, 1), rb_send.at[at], rb_recv.at[at], at_lo(far))
 
-    for step in range(1, n_ctx):
-        z_copies[step - 1].wait_recv()
-        owner = down(c, n_ctx, step)
-        for part in range(2):
-            for hop in range(1, n_lo):
-                at = (step - 1, hop - 1, part)
-                lo_copies[at] = move(share(owner, v, part), lo_send.at[at], lo_recv.at[at], at_lo(hop))
-            for hop in range(1, n_hi):
-                at = (step - 1, hop - 1, 1 - part)
-                hi_copies[at] = move(share(owner, v, 1 - part), hi_send.at[at], hi_recv.at[at], at_hi(hop))
-        if step >= 2:
-            relay(step - 1)
-    relay(n_ctx - 1)
-    for step in range(1, n_ctx):
+    def finish(step):
         for copies in (lo_copies, hi_copies):
             for at, copy in copies.items():
                 if at[0] == step - 1 and at[2] == (1 if copies is lo_copies else 0):
@@ -179,6 +167,24 @@
             if at[0] == step:
                 copy.wait_recv()
         do_block(down(c, n_ctx, step))
+
+    for step in range(1, n_ctx):
+        owner = down(c, n_ctx, step)
+        for part in range(2):
+            z_copies[step - 1, part].wait_recv()
+            for hop in range(1, n_lo):
+                at = (step - 1, hop - 1, part)
+                lo_copies[at] = move(share(owner, v, part), lo_send.at[at], lo_recv.at[at], at_lo(hop))
+            for hop in range(1, n_hi):
+                at = (step - 1, hop - 1, part)
+                hi_copies[at] = move(share(owner, v, part), hi_send.at[at], hi_recv.at[at], at_hi(hop))
+        if step >= 2:
+            relay(step - 1)
+        if step >= 3:
+            finish(step - 2)
+    relay(n_ctx - 1)
+    for step in range(max(1, n_ctx - 2), n_ctx):
+        finish(step)
 
     store_h = pltpu.make_async_copy(hbuf, hid_all.at[g], local_sem.at[2])
     store_h.start()
@@ -374,7 +380,7 @@
             pltpu.VMEM((n_ctx, out_rows, depth), bf16),
             pltpu.VMEM((n_ctx - 1, out_rows, depth), bf16),
             dma((4,)),
-            dma((n_ctx - 1,)), dma((n_ctx - 1,)),
+            dma((n_ctx - 1, 2)), dma((n_ctx - 1, 2)),
             dma((n_ctx - 1, wide, 2)), dma((n_ctx - 1, wide, 2)),
             dma((n_ctx - 1, wide, 2)), dma((n_ctx - 1, wide, 2)),
             dma((n_ctx - 1, wide, wide)), dma((n_ctx - 1, wide, wide)),

time: 75.1 us -> 74.6 us (level)
  no operation moved by 1% of the time
where the time goes in v4:
time: 74.6 us; the launch traced here: 74.4 us
  Pallas kernels  65.7 us (88%)
  matrix products  7.39 us (10%)
    pallas_call x1, Pallas kernels, per_device(): pl.pallas_call(functools.partial(kernel, n_dp, n_ctx, n_hi, n_lo), out_sh...  65.7 us
    dot_general x1, matrix products, per_device(): lax.dot_general(grad_all.reshape(n_dp * tokens, width), hid_all.reshape(n...  7.39 us

profile of v4, /device:TPU:0, one launch (start us, length us, event | category | flops | bytes accessed | tf_op | source)
XLA Modules:
  0.0 74.4 jit_solution(5445248426983034084)
XLA Ops:
  0.6 65.7 %shard_map.95 = (bf16[16,4096]{1,0:T(8,128)(2,1)}, bf16[2,256,4096]{2,1,0:T(8,128)(2,1)}, bf16[2,256,594]{2,1,0:T(8,128)(2,1)}) custom-call(bf16[64,4096]{1,0:T(8,128)(2,1)} %hid.1, bf16[594,4096]{1,0:T(8,128)(2,1)} %bitcast.9, s32[32]{0:T(128)} %lengths.1, f32[32]{0:T(128)} %advantages.1, s32[1,256]{1,0:T(1,128)} %bitcast.10, s32[1,256]{1,0:T(1,128)} %bitcast.11, ...), custom_call_target="tpu_custom_call" | custom-call | tf_op jit(solution)/shard_map/pallas_call | solution.py:354
  66.4 0.0 copy-start
  66.4 7.4 %bitcast_convert_fusion = bf16[4096,594]{0,1:T(8,128)(2,1)} fusion(bf16[2,256,4096]{2,1,0:T(8,128)(2,1)} %get-tuple-element.6, bf16[2,256,594]{2,1,0:T(8,128)(2,1)} %get-tuple-element.7), kind=kOutput, calls=%fused_computation | convolution fusion | flops 2493849600 | bytes 9668608 | tf_op jit(solution)/shard_map/dot_general | solution.py:400
  73.8 0.0 copy-done
  73.8 0.7 copy.13
Async XLA Ops:
  66.4 7.4 %copy-start = (bf16[16,4096]{1,0:T(8,128)(2,1)S(1)}, bf16[16,4096]{1,0:T(8,128)(2,1)}, u32[]{:S(2)}) copy-start(bf16[16,4096]{1,0:T(8,128)(2,1)} %get-tuple-element.10) | copy-start | bytes 393220
